TPU v7x, 512 devices: a whole 4x8x8 slice. The times are simulated.
512 devices in a mesh: grp: 16 (over y, core), seq: 32 (over z, x).
Axes of the slice: x: 4, y: 8, z: 8, core: 2. Of those that a mesh axis runs over, the one named last changes fastest.
Arguments:
- attention_output: bfloat16 [8192, 8192], P('grp', 'seq'), may hold values from -6 to 6
- output_gradient: bfloat16 [8192, 8192], P('grp', 'seq'), may hold values from -6 to 6
- output_projection_weight: bfloat16 [8192, 8192], P('seq', 'grp'), may hold values from -0.0625 to 0.0625
- tenant_down_factors: bfloat16 [32, 64, 8192], P(None, None, 'seq'), may hold values from -0.0625 to 0.0625
- tenant_up_factors: bfloat16 [32, 64, 8192], P(None, None, 'seq'), may hold values from -0.0625 to 0.0625
- block_tenant_index: int32 [64], replicated, may hold values from 0 to 31, as said below
- block_valid_rows: int32 [64], replicated, may hold values from 16 to 128, as said below
- tenant_output_row: int32 [32], replicated, may hold values from 0 to 31, as said below
Outputs:
- attention_gradient: bfloat16 [8192, 8192], P('grp', 'seq')
- grad_down: float32 [32, 64, 8192], P('grp', None, 'seq')
- grad_up: float32 [32, 64, 8192], P('grp', None, 'seq')
Inputs may be any that keep to these rules, and one draw needn't show every extreme that they name: `block_tenant_index`: the 4 blocks of one group belong to different tenants whose groups tenant_output_row[t] // 2 differ; in every draw one group keeps a tenant of one block of every group. `block_valid_rows`: in every group one block has all 128 rows valid. `tenant_output_row`: A permutation of the tenants.
All inputs are finite; a program needn't handle non-finite values.
Results may differ from a plain program's by a relative error of at most 0.0031.
Values may be sent and summed in bfloat16 or wider, within the bound.
A program may use at most 64 MiB of HBM per device.

v0:
```python
import jax
import jax.numpy as jnp
from jax import lax
from jax.sharding import PartitionSpec as P

BLOCK = 128
adapter_scale = 2.0


def shards(
    attention_output,
    output_gradient,
    output_projection_weight,
    tenant_down_factors,
    tenant_up_factors,
    block_tenant_index,
    block_valid_rows,
    tenant_output_row,
):
    group_index = lax.axis_index("grp")
    rows_group, head_cols = attention_output.shape
    col_width = output_gradient.shape[1]
    blocks = rows_group // BLOCK
    tenants = tenant_output_row.shape[0]
    place_all = jnp.sum(
        jnp.where(
            block_tenant_index[:, None] == jnp.arange(tenants, dtype=jnp.int32)[None, :],
            tenant_output_row[None, :],
            0,
        ),
        axis=1,
    )
    local_tenants = lax.dynamic_slice_in_dim(block_tenant_index, group_index * blocks, blocks)
    my_counts = lax.dynamic_slice_in_dim(block_valid_rows, group_index * blocks, blocks)
    my_places = lax.dynamic_slice_in_dim(place_all, group_index * blocks, blocks)
    positions = jnp.arange(rows_group, dtype=jnp.int32)
    block_of = positions // BLOCK
    limits = jnp.sum(
        jnp.where(
            jnp.arange(blocks, dtype=jnp.int32)[None, :] == block_of[:, None], my_counts[None, :], 0
        ),
        axis=1,
    )
    masked = jnp.where(
        (positions % BLOCK < limits)[:, None], output_gradient, jnp.zeros((), jnp.bfloat16)
    )
    contract_rows = (((1,), (1,)), ((), ()))
    weight_rows = lax.all_gather(output_projection_weight, "grp", axis=1, tiled=True)
    frozen_input_gradient = lax.dot_general(
        lax.all_gather(masked, "seq", axis=1, tiled=True),
        weight_rows,
        contract_rows,
        preferred_element_type=jnp.float32,
    )
    adapter_down_factor = tenant_down_factors[local_tenants]
    adapter_up_factor = tenant_up_factors[local_tenants]
    hidden_row_blocks = attention_output.reshape(blocks, BLOCK, head_cols)
    gradient_row_blocks = masked.reshape(blocks, BLOCK, col_width)
    down_part = jnp.einsum(
        "bkh,brh->bkr", hidden_row_blocks, adapter_down_factor, preferred_element_type=jnp.float32
    )
    grad_part = jnp.einsum(
        "ejz,elz->ejl", gradient_row_blocks, adapter_up_factor, preferred_element_type=jnp.float32
    )
    down_sum, grad_sum = lax.psum((down_part, grad_part), "seq")
    down_rank_product = down_sum.astype(jnp.bfloat16)
    rank_gradient = grad_sum.astype(jnp.bfloat16)
    adapter_branch_term = jnp.einsum(
        "wtf,wfl->wtl", rank_gradient, adapter_down_factor, preferred_element_type=jnp.float32
    ).reshape(rows_group, head_cols)
    attention_gradient = (frozen_input_gradient + adapter_scale * adapter_branch_term).astype(
        jnp.bfloat16
    )
    down_gradient_panel = adapter_scale * jnp.einsum(
        "eit,eiz->etz", rank_gradient, hidden_row_blocks, preferred_element_type=jnp.float32
    )
    up_gradient_panel = adapter_scale * jnp.einsum(
        "jlx,jln->jxn", down_rank_product, gradient_row_blocks, preferred_element_type=jnp.float32
    )
    panels = jnp.concatenate([down_gradient_panel, up_gradient_panel], axis=2)
    select = (jnp.arange(tenants, dtype=jnp.int32)[:, None] == my_places[None, :]).astype(
        jnp.float32
    )
    spread = jnp.einsum(
        "pb,brx->prx",
        select,
        panels,
        precision=lax.Precision.HIGHEST,
        preferred_element_type=jnp.float32,
    )
    summed = lax.psum_scatter(spread, "grp", scatter_dimension=0, tiled=True)
    grad_down = summed[:, :, :head_cols]
    grad_up = summed[:, :, head_cols:]
    return (attention_gradient, grad_down, grad_up)


def solution(mesh):
    placed = (
        P("grp", "seq"),
        P("grp", "seq"),
        P("seq", "grp"),
        P(None, None, "seq"),
        P(None, None, "seq"),
        P(),
        P(),
        P(),
    )
    return jax.shard_map(
        shards,
        mesh=mesh,
        in_specs=placed,
        out_specs=(P("grp", "seq"), P("grp", None, "seq"), P("grp", None, "seq")),
        check_vma=False,
    )
```

profile of v0, /device:TPU:8, one launch (start us, length us, event | category | flops | bytes accessed | tf_op | source)
XLA Modules:
  0.0 403.3 jit_solution(14572246744692483261)
XLA Ops:
  7.2 0.0 copy-start
  7.2 0.0 reduce-scatter.2.cloned.1.call-start
  7.2 0.8 dynamic_slice.9
  8.1 0.1 select_reduce_fusion.1
  8.1 0.7 compare_select_fusion
  8.9 1.1 broadcast_select_fusion
  10.0 0.0 copy-start.1
  10.0 0.0 copy-done
  10.0 0.6 gather_fusion
  10.6 0.2 fusion.16
  10.8 1.8 gather_fusion.1
  12.6 1.1 convolution_bitcast_fusion
  13.7 150.4 %all-reduce.2 = (bf16[4,128,64]{1,2,0:T(8,128)(2,1)S(1)}, bf16[4,128,64]{1,2,0:T(8,128)(2,1)S(1)}) all-reduce(f32[4,128,64]{1,2,0:T(8,128)S(1)} %fusion.16, f32[4,128,64]{1,2,0:T(8,128)S(1)} %convolution_bitcast_fusion), channel_id=1, replica_groups=mesh['grp'=16,'seq'=32] {'seq'}, use_global_device_ids=true, to_apply=%region_1.2 | all-reduce | flops 65536 | bytes 393216 | tf_op jit(solution)/shard_map/psum | solution.py:65
  164.1 0.2 convolution_multiply_fusion.1
  164.3 1.1 convolution_multiply_fusion.2
  165.4 0.8 select_reduce_fusion
  166.2 0.1 dynamic_slice.11
  166.2 0.1 pad_maximum_fusion
  166.3 2.0 fusion.1
  168.3 0.0 copy-done.1
  168.3 4.4 %copy.15 = f32[32,64,512]{2,1,0:T(8,128)} copy(f32[32,64,512]{2,0,1:T(8,128)S(1)} %fusion.1) | data formatting | bytes 8388608 | tf_op jit(solution)/shard_map/pb,brx->prx/dot_general | solution.py:84
  172.7 0.0 reduce-scatter.2.cloned.1.call-update
  172.7 0.0 all-gather.5.cloned.1.call-start
  172.8 0.7 all-gather.5.cloned.1.call-update
  173.5 0.0 all-gather.3.cloned.1.call-start
  173.5 0.7 all-gather.3.cloned.1.call-update
  174.2 0.3 convolution_multiply_fusion
  174.5 55.3 %reduce-scatter.2.cloned.1.call-done = f32[2,64,512]{2,1,0:T(8,128)} async-done(((f32[32,64,512]{2,1,0:T(8,128)}), f32[2,64,512]{2,1,0:T(8,128)}) %reduce-scatter.2.cloned.1.call-update) | async-done | bytes 262160 | tf_op jit(solution)/shard_map/reduce_scatter | solution.py:91
  229.8 1.7 fusion.15
  231.5 47.0 %all-gather.5.cloned.1.call-done = bf16[256,8192]{1,0:T(8,128)(2,1)} async-done(((bf16[256,512]{1,0:T(8,128)(2,1)}), bf16[256,8192]{1,0:T(8,128)(2,1)}) %all-gather.5.cloned.1.call-update) | async-done | bytes 4194320 | tf_op jit(solution)/shard_map/all_gather | solution.py:48
  278.4 110.7 %all-gather.3.cloned.1.call-done = bf16[512,8192]{1,0:T(8,128)(2,1)} async-done(((bf16[512,256]{1,0:T(8,128)(2,1)}), bf16[512,8192]{1,0:T(8,128)(2,1)}) %all-gather.3.cloned.1.call-update) | async-done | bytes 8388624 | tf_op jit(solution)/shard_map/all_gather | solution.py:50
  389.2 7.6 %fusion = bf16[512,256]{1,0:T(8,128)(2,1)} fusion(f32[512,256]{1,0:T(8,128)S(1)} %bitcast.24, bf16[512,8192]{1,0:T(8,128)(2,1)} %all-gather.3.cloned.1.call-done, bf16[256,8192]{1,0:T(8,128)(2,1)} %all-gather.5.cloned.1.call-done), kind=kOutput, calls=%fused_computation.4 | convolution fusion | flops 2147745792 | bytes 13369344 | tf_op jit(solution)/shard_map/dot_general | solution.py:49
  (3 shorter events, 0.0 us)
Async XLA Ops:
  7.2 2.8 copy-start
  7.2 222.6 %reduce-scatter.2.cloned.1.call-start = ((), (), s32[]{:S(2)}) async-start(), calls=%async_computation.3 | async-start | bytes 4456448 | tf_op jit(solution)/shard_map/reduce_scatter | solution.py:91
  10.0 158.3 %copy-start.1 = (bf16[512,256]{1,0:T(8,128)(2,1)}, bf16[512,256]{1,0:T(8,128)(2,1)S(1)}, u32[]{:S(2)}) copy-start(bf16[512,256]{1,0:T(8,128)(2,1)S(1)} %broadcast_select_fusion) | copy-start | bytes 786436
  172.7 105.7 %all-gather.5.cloned.1.call-start = ((), (), s32[]{:S(2)}) async-start(), calls=%async_computation.2 | async-start | bytes 4456448 | tf_op jit(solution)/shard_map/all_gather | solution.py:48
  173.5 215.7 %all-gather.3.cloned.1.call-start = ((), (), s32[]{:S(2)}) async-start(), calls=%async_computation.1 | async-start | bytes 8650752 | tf_op jit(solution)/shard_map/all_gather | solution.py:50
Sparse Core Ops, SparseCore 0:
  172.8 56.8 reduce-scatter.1
  231.9 46.4 all-gather.4
  282.0 107.0 all-gather.2
where the time goes:
time: 404 us; the launch traced here: 403 us
  waiting for transfers between devices  214 us (53%)
  blocking collectives  150 us (37%)
  between operations  13.9 us (3%)
  matrix products  12.5 us (3%)
  local copies, waits for them, and re-layouts  9.3 us (2%)
    psum x1, blocking collectives, shards(): down_sum, grad_sum = lax.psum((down_part, grad_part), 'seq')  150 us
    all_gather x1, waiting for transfers between devices, shards(): lax.all_gather(masked, 'seq', axis=1, tiled=True)  111 us
    reduce_scatter x1, waiting for transfers between devices, shards(): summed = lax.psum_scatter(spread, 'grp', scatter_dimension=0, tiled=True)  55.3 us
    all_gather x1, waiting for transfers between devices, shards(): lax.all_gather(output_projection_weight, 'grp', axis=1, tiled=True)  47 us
  transfers between devices with their start and end apart: 3, of which 3 were waited for; matrix products, arithmetic and copies ran while one was open for 0% of the time, Pallas kernels for 0%

commit v1 on v0

--- a/solution.py
+++ b/solution.py
@@ -45,7 +45,10 @@
         (positions % BLOCK < limits)[:, None], output_gradient, jnp.zeros((), jnp.bfloat16)
     )
     contract_rows = (((1,), (1,)), ((), ()))
-    weight_rows = lax.all_gather(output_projection_weight, "grp", axis=1, tiled=True)
+    weight_rows = jnp.concatenate(
+        lax.all_to_all(jnp.stack([output_projection_weight] * lax.axis_size("grp")), "grp", 0, 0),
+        axis=1,
+    )
     frozen_input_gradient = lax.dot_general(
         lax.all_gather(masked, "seq", axis=1, tiled=True),
         weight_rows,

time: 404 us -> 325 us (0.80)
  the two profiles are of different devices: /device:TPU:8 before, /device:TPU:29 now
where the time goes in v1:
time: 325 us
  waiting for transfers between devices  128 us (39%)
  blocking collectives  118 us (36%)
  starting transfers between devices  35.8 us (11%)
  between operations  15.6 us (5%)
  matrix products  12.5 us (4%)
  local copies, waits for them, and re-layouts  12.1 us (4%)
    reduce_scatter x1, waiting for transfers between devices, shards(): summed = lax.psum_scatter(spread, 'grp', scatter_dimension=0, tiled=True)  127 us
    psum x1, blocking collectives, shards(): down_sum, grad_sum = lax.psum((down_part, grad_part), 'seq')  118 us
    all_to_all x1, starting transfers between devices, shards(): lax.all_to_all(jnp.stack([output_projection_weight] * lax.axis_size('grp'...  35.7 us
    dot_general x1, matrix products, shards(): lax.dot_general(lax.all_gather(masked, 'seq', axis=1, tiled=True), weight...  7.61 us
  transfers between devices with their start and end apart: 3, of which 1 were waited for; matrix products, arithmetic and copies ran while one was open for 1% of the time, Pallas kernels for 0%

profile of v1, /device:TPU:29, one launch (start us, length us, event | category | flops | bytes accessed | tf_op | source)
XLA Modules:
  0.0 324.8 jit_solution(16980761010399063740)
XLA Ops:
  8.0 0.0 copy-start
  8.0 0.0 reduce-scatter.2.cloned.1.call-start
  8.1 0.8 dynamic_slice.9
  8.9 0.7 compare_select_fusion
  9.6 0.8 select_reduce_fusion
  10.4 0.1 dynamic_slice.11
  10.5 0.1 select_reduce_fusion.1
  10.6 0.0 copy-done
  10.6 0.6 gather_fusion.1
  11.1 1.8 gather_fusion
  12.9 1.1 convolution_bitcast_fusion
  14.1 1.1 broadcast_select_fusion
  15.2 0.0 copy-start.1
  15.2 0.2 fusion.16
  15.4 118.0 %all-reduce.2 = (bf16[4,128,64]{1,2,0:T(8,128)(2,1)S(1)}, bf16[4,128,64]{1,2,0:T(8,128)(2,1)S(1)}) all-reduce(f32[4,128,64]{1,2,0:T(8,128)S(1)} %fusion.16, f32[4,128,64]{1,2,0:T(8,128)S(1)} %convolution_bitcast_fusion), channel_id=1, replica_groups=mesh['grp'=16,'seq'=32] {'seq'}, use_global_device_ids=true, to_apply=%region_1.2 | all-reduce | flops 65536 | bytes 393216 | tf_op jit(solution)/shard_map/psum | solution.py:68
  133.4 0.2 convolution_multiply_fusion.1
  133.6 1.1 convolution_multiply_fusion.2
  134.7 0.1 pad_maximum_fusion
  134.8 2.0 fusion.1
  136.8 4.4 %copy.21 = f32[32,64,512]{2,1,0:T(8,128)} copy(f32[32,64,512]{2,0,1:T(8,128)S(1)} %fusion.1) | data formatting | bytes 8388608 | tf_op jit(solution)/shard_map/pb,brx->prx/dot_general | solution.py:87
  141.1 0.0 copy-done.1
  141.1 0.0 copy-start.2
  141.1 0.0 reduce-scatter.2.cloned.1.call-update
  141.2 0.0 all-gather.2.cloned.1.call-start
  141.2 0.5 all-gather.2.cloned.1.call-update
  141.7 0.3 copy-done.2
  142.1 0.1 copy.19
  142.2 2.3 stack.2
  144.6 35.7 %all-to-all-start = ((bf16[16,256,512]{1,2,0:T(8,128)(2,1)}), bf16[16,256,512]{1,2,0:T(8,128)(2,1)}, u32[]{:S(2)}, u32[]{:S(2)}) async-start(bf16[16,256,512]{1,2,0:T(8,128)(2,1)} %stack.2), calls=%async_computation | async-start | bytes 8388608 | tf_op jit(solution)/shard_map/all_to_all | solution.py:49
  180.3 0.3 convolution_multiply_fusion
  180.6 127.4 %reduce-scatter.2.cloned.1.call-done = f32[2,64,512]{2,1,0:T(8,128)} async-done(((f32[32,64,512]{2,1,0:T(8,128)}), f32[2,64,512]{2,1,0:T(8,128)}) %reduce-scatter.2.cloned.1.call-update) | async-done | bytes 262160 | tf_op jit(solution)/shard_map/reduce_scatter | solution.py:94
  308.0 1.7 fusion.15
  309.7 0.0 all-to-all-done
  309.7 0.0 all-gather.2.cloned.1.call-done
  309.7 7.6 %fusion = bf16[512,256]{1,0:T(8,128)(2,1)} fusion(f32[512,256]{1,0:T(8,128)S(1)} %bitcast.27, bf16[512,8192]{1,0:T(8,128)(2,1)} %all-gather.2.cloned.1.call-done, bf16[256,8192]{0,1:T(8,128)(2,1)} %bitcast.1), kind=kOutput, calls=%fused_computation.4 | convolution fusion | flops 2147745792 | bytes 13369344 | tf_op jit(solution)/shard_map/dot_general | solution.py:52
  (3 shorter events, 0.0 us)
Async XLA Ops:
  8.0 2.6 copy-start
  8.0 300.0 %reduce-scatter.2.cloned.1.call-start = ((), (), s32[]{:S(2)}) async-start(), calls=%async_computation.3 | async-start | bytes 4456448 | tf_op jit(solution)/shard_map/reduce_scatter | solution.py:94
  15.2 126.0 %copy-start.1 = (bf16[512,256]{1,0:T(8,128)(2,1)}, bf16[512,256]{1,0:T(8,128)(2,1)S(1)}, u32[]{:S(2)}) copy-start(bf16[512,256]{1,0:T(8,128)(2,1)S(1)} %broadcast_select_fusion) | copy-start | bytes 786436
  141.1 1.0 copy-start.2
  141.2 168.5 %all-gather.2.cloned.1.call-start = ((), (), s32[]{:S(2)}) async-start(), calls=%async_computation.2 | async-start | bytes 8650752 | tf_op jit(solution)/shard_map/all_gather | solution.py:53
  144.6 165.1 %all-to-all-start = ((bf16[16,256,512]{1,2,0:T(8,128)(2,1)}), bf16[16,256,512]{1,2,0:T(8,128)(2,1)}, u32[]{:S(2)}, u32[]{:S(2)}) async-start(bf16[16,256,512]{1,2,0:T(8,128)(2,1)} %stack.2), calls=%async_computation | async-start | bytes 8388608 | tf_op jit(solution)/shard_map/all_to_all | solution.py:49
Sparse Core Ops, SparseCore 0:
  141.3 166.6 reduce-scatter.1
Sparse Core Ops, SparseCore 1:
  145.3 130.7 all-gather.1
